TPU v7x, 32 devices: a whole 2x2x4 slice. The times are simulated.
32 devices in a mesh: layer: 2 (over y), row: 4 (over z), col: 4 (over x, core).
Axes of the slice: x: 2, y: 2, z: 4, core: 2. Of those that a mesh axis runs over, the one named last changes fastest.
Arguments:
- right_side: float32 [16, 4, 64, 128], P(None, 'row', 'layer'), may hold values from -6 to 6
- below: float32 [2, 16, 4, 64, 128], P('layer', None, 'row'), may hold values from -4 to 4
- diag_inverse: float32 [4, 4, 4, 4, 4, 128, 128], P(None, None, 'row', None, 'col'), as said below
- factor_blocks: float32 [4, 4, 4, 128, 128], P('row', 'col'), may hold values from -0.125 to 0.125
- block_row: int32 [4, 4, 4], P('row', 'col'), may hold values from 16 to 63, as said below
- block_col: int32 [4, 4, 4], P('row', 'col'), may hold values from 0 to 47, as said below
Outputs:
- solution: float32 [16, 4, 64, 128], P(None, 'row', 'layer')
Inputs may be any that keep to these rules, and one draw needn't show every extreme that they name: block_row[r, c, n] % 4 == r. block_col[r, c, n] % 4 == c, and block_col[r, c, n] // 16 < block_row[r, c, n] // 16. `diag_inverse`: blocks with k < m are zero and blocks with k == m are lower triangular; the diagonal entries of the diagonal blocks lie in 0.5 to 1.5; the other entries below the diagonal are of mean zero with a spread of about 0.5 / sqrt(128) inside the diagonal blocks and 0.5 / sqrt(2048) in the blocks with k > m, not bounded.
All inputs are finite; a program needn't handle non-finite values.
Results may differ from a plain program's by a relative error of at most 0.0001.
Values sent between devices are 32-bit elements; how exact they have to be, the bound alone decides.
A program may use at most 64 MiB of HBM per device.

v0:
```python
import jax
import jax.numpy as jnp
from jax import lax
from jax.sharding import PartitionSpec as P

BLK = 128
NB = 16
STEPS = 4


def body(right_side, below, diag_inverse, factor_blocks, block_row, block_col):
    rows_count = lax.axis_size("row")
    cols_count = lax.axis_size("col")
    col_self = lax.axis_index("col")
    own_rhs = right_side[:, 0]
    local_rows = own_rhs.shape[0]
    rhs_width = own_rhs.shape[1]
    each_supernode_list = NB // rows_count
    col_width = NB // cols_count
    listed = factor_blocks[0, 0]
    row_index = block_row[0, 0]
    col_index = block_col[0, 0]
    row_onehot = (row_index[:, None] // rows_count == jnp.arange(local_rows)[None, :]).astype(
        jnp.float32
    )
    inverted_diagonal = diag_inverse[:, :, 0, :, 0]
    merged = own_rhs - lax.psum_scatter(below[0, :, 0], "layer", scatter_dimension=1, tiled=True)
    accumulated = jnp.zeros_like(own_rhs)
    solved_pieces = []
    for current_supernode in range(STEPS):
        first_row = current_supernode * each_supernode_list
        last_row = first_row + each_supernode_list
        merged_part = merged[first_row:last_row]
        offset = col_index - current_supernode * NB
        active = ((offset >= 0) & (offset < NB)).astype(jnp.float32)
        summed = lax.psum(accumulated[first_row:last_row], "col")
        target_rows = merged_part - summed
        relayed = lax.all_gather(target_rows[:, None], "row", axis=1, tiled=True).reshape(
            NB, rhs_width, BLK
        )
        local_target_rows = lax.dynamic_index_in_dim(
            relayed.reshape(col_width, cols_count, rhs_width, BLK), col_self, 1, keepdims=False
        )
        partial_solved = jnp.einsum(
            "exnc,xvc->evn",
            inverted_diagonal[current_supernode],
            local_target_rows,
            precision=lax.Precision.HIGHEST,
        )
        solved_own = lax.psum(partial_solved, "col")
        if current_supernode + 1 < STEPS:
            solved_all = lax.all_gather(solved_own[:, None], "row", axis=1, tiled=True).reshape(
                NB, rhs_width, BLK
            )
            chosen = jnp.take(solved_all, jnp.clip(offset, 0, NB - 1), axis=0)
        solved_pieces.append(solved_own)
        if current_supernode + 1 < STEPS:
            products = jnp.einsum("nrb,nab->nra", chosen, listed, precision=lax.Precision.HIGHEST)
            accumulated = accumulated + jnp.einsum(
                "nq,nra->qra",
                row_onehot * active[:, None],
                products,
                precision=lax.Precision.HIGHEST,
            )
    solution = jnp.concatenate(solved_pieces, axis=0)
    return solution[:, None]


def solution(mesh):
    return jax.shard_map(
        body,
        mesh=mesh,
        in_specs=(
            P(None, "row", "layer", None),
            P("layer", None, "row", None, None),
            P(None, None, "row", None, "col", None, None),
            P("row", "col", None, None, None),
            P("row", "col", None),
            P("row", "col", None),
        ),
        out_specs=P(None, "row", "layer", None),
        check_vma=False,
    )
```

profile of v0, /device:TPU:0, one launch (start us, length us, event | category | flops | bytes accessed | tf_op | source)
XLA Modules:
  0.0 379.0 jit_solution(7818879516390627955)
XLA Ops:
  6.5 2.2 copy.56
  8.8 0.7 and_select_fusion
  9.5 0.7 fusion.37
  10.1 0.7 compare_and_fusion
  10.8 16.2 %reduce-scatter.2.cloned.1.call-done = f32[16,32,128]{2,0,1:T(8,128)} async-done(((f32[16,64,128]{2,0,1:T(8,128)}), f32[16,32,128]{2,0,1:T(8,128)}) %reduce-scatter.2.cloned.1.call-update) | async-done | bytes 262160 | tf_op jit(solution)/shard_map/reduce_scatter | solution.py:27
  27.0 1.2 bitcast_subtract_fusion
  28.2 13.9 %all-gather = f32[4,128,128]{2,0,1:T(4,128)S(1)} all-gather(f32[4,32,128]{2,0,1:T(4,128)S(1)} %slice.55), channel_id=2, replica_groups=mesh['layer'=2,'row'=4,'col'=4] {'row'}, dimensions={1}, use_global_device_ids=true | all-gather | bytes 327680 | tf_op jit(solution)/shard_map/all_gather | solution.py:38
  42.1 2.9 convolution_bitcast_fusion.3
  45.1 32.2 %all-reduce.8.cloned.1.call-done = f32[4,32,128]{2,1,0:T(8,128)} async-done(((f32[4,32,128]{2,1,0:T(8,128)}), f32[4,32,128]{2,1,0:T(8,128)}) %all-reduce.8.cloned.1.call-update) | async-done | bytes 65552 | tf_op jit(solution)/shard_map/psum | solution.py:50
  77.3 14.1 %all-gather.1 = f32[4,128,128]{2,1,0:T(8,128)S(1)} all-gather(f32[4,32,128]{2,1,0:T(8,128)} %all-reduce.8.cloned.1.call-done), channel_id=3, replica_groups=mesh['layer'=2,'row'=4,'col'=4] {'row'}, dimensions={1}, use_global_device_ids=true | all-gather | bytes 327680 | tf_op jit(solution)/shard_map/all_gather | solution.py:52
  93.0 0.6 slice.58
  93.8 31.8 %all-reduce.10.cloned.1.call-done = f32[4,32,128]{2,0,1:T(4,128)} async-done(((f32[4,32,128]{2,0,1:T(4,128)}), f32[4,32,128]{2,0,1:T(4,128)}) %all-reduce.10.cloned.1.call-update) | async-done | bytes 65552 | tf_op jit(solution)/shard_map/psum | solution.py:36
  125.5 0.9 slice_subtract_fusion.2
  126.4 13.9 %all-gather.2 = f32[4,128,128]{2,0,1:T(4,128)S(1)} all-gather(f32[4,32,128]{2,0,1:T(4,128)S(1)} %slice_subtract_fusion.2), channel_id=4, replica_groups=mesh['layer'=2,'row'=4,'col'=4] {'row'}, dimensions={1}, use_global_device_ids=true | all-gather | bytes 327680 | tf_op jit(solution)/shard_map/all_gather | solution.py:38
  140.3 2.9 convolution_bitcast_fusion.2
  143.3 31.8 %all-reduce.12.cloned.1.call-done = f32[4,32,128]{2,1,0:T(8,128)} async-done(((f32[4,32,128]{2,1,0:T(8,128)}), f32[4,32,128]{2,1,0:T(8,128)}) %all-reduce.12.cloned.1.call-update) | async-done | bytes 65552 | tf_op jit(solution)/shard_map/psum | solution.py:50
  175.0 14.2 %all-gather.3 = f32[4,128,128]{2,1,0:T(8,128)S(1)} all-gather(f32[4,32,128]{2,1,0:T(8,128)} %all-reduce.12.cloned.1.call-done), channel_id=5, replica_groups=mesh['layer'=2,'row'=4,'col'=4] {'row'}, dimensions={1}, use_global_device_ids=true | all-gather | bytes 327680 | tf_op jit(solution)/shard_map/all_gather | solution.py:52
  190.9 0.6 slice.61
  191.6 31.8 %all-reduce.14.cloned.1.call-done = f32[4,32,128]{2,0,1:T(4,128)} async-done(((f32[4,32,128]{2,0,1:T(4,128)}), f32[4,32,128]{2,0,1:T(4,128)}) %all-reduce.14.cloned.1.call-update) | async-done | bytes 65552 | tf_op jit(solution)/shard_map/psum | solution.py:36
  223.4 0.9 slice_subtract_fusion.1
  224.2 13.9 %all-gather.4 = f32[4,128,128]{2,0,1:T(4,128)S(1)} all-gather(f32[4,32,128]{2,0,1:T(4,128)S(1)} %slice_subtract_fusion.1), channel_id=6, replica_groups=mesh['layer'=2,'row'=4,'col'=4] {'row'}, dimensions={1}, use_global_device_ids=true | all-gather | bytes 327680 | tf_op jit(solution)/shard_map/all_gather | solution.py:38
  238.1 2.9 convolution_bitcast_fusion.1
  241.1 31.8 %all-reduce.16.cloned.1.call-done = f32[4,32,128]{2,1,0:T(8,128)} async-done(((f32[4,32,128]{2,1,0:T(8,128)}), f32[4,32,128]{2,1,0:T(8,128)}) %all-reduce.16.cloned.1.call-update) | async-done | bytes 65552 | tf_op jit(solution)/shard_map/psum | solution.py:50
  272.8 14.1 %all-gather.5 = f32[4,128,128]{2,1,0:T(8,128)S(1)} all-gather(f32[4,32,128]{2,1,0:T(8,128)} %all-reduce.16.cloned.1.call-done), channel_id=7, replica_groups=mesh['layer'=2,'row'=4,'col'=4] {'row'}, dimensions={1}, use_global_device_ids=true | all-gather | bytes 327680 | tf_op jit(solution)/shard_map/all_gather | solution.py:52
  287.5 0.6 fusion
  288.6 0.7 slice_add_fusion
  289.3 31.8 %all-reduce.18.cloned.1.call-done = f32[4,32,128]{2,0,1:T(4,128)} async-done(((f32[4,32,128]{2,0,1:T(4,128)}), f32[4,32,128]{2,0,1:T(4,128)}) %all-reduce.18.cloned.1.call-update) | async-done | bytes 65552 | tf_op jit(solution)/shard_map/psum | solution.py:36
  321.1 0.9 slice_subtract_fusion
  321.9 13.9 %all-gather.6 = f32[4,128,128]{2,0,1:T(4,128)S(1)} all-gather(f32[4,32,128]{2,0,1:T(4,128)S(1)} %slice_subtract_fusion), channel_id=8, replica_groups=mesh['layer'=2,'row'=4,'col'=4] {'row'}, dimensions={1}, use_global_device_ids=true | all-gather | bytes 327680 | tf_op jit(solution)/shard_map/all_gather | solution.py:38
  335.8 2.9 convolution_bitcast_fusion
  338.7 31.8 %all-reduce.20.cloned.1.call-done = f32[4,32,128]{2,1,0:T(8,128)} async-done(((f32[4,32,128]{2,1,0:T(8,128)}), f32[4,32,128]{2,1,0:T(8,128)}) %all-reduce.20.cloned.1.call-update) | async-done | bytes 65552 | tf_op jit(solution)/shard_map/psum | solution.py:50
  370.5 1.6 maximum_bitcast_fusion
  (38 shorter events, 4.9 us)
Async XLA Ops:
  6.5 85.4 %copy-start = (f32[1,1,4,128,128]{4,3,2,1,0:T(8,128)S(1)}, f32[1,1,4,128,128]{4,3,2,1,0:T(8,128)}, u32[]{:S(2)}) copy-start(f32[1,1,4,128,128]{4,3,2,1,0:T(8,128)} %param.11) | copy-start | bytes 786436
  6.5 20.4 %reduce-scatter.2.cloned.1.call-start = ((), (), s32[]{:S(2)}) async-start(), calls=%async_computation.1 | async-start | bytes 786432 | tf_op jit(solution)/shard_map/reduce_scatter | solution.py:27
  8.7 68.6 %all-reduce.8.cloned.1.call-start = ((), (), s32[]{:S(2)}) async-start(), calls=%async_computation.2 | async-start | bytes 131072 | tf_op jit(solution)/shard_map/psum | solution.py:50
  45.0 80.5 %all-reduce.10.cloned.1.call-start = ((), (), s32[]{:S(2)}) async-start(), calls=%async_computation.3 | async-start | bytes 131072 | tf_op jit(solution)/shard_map/psum | solution.py:36
  93.7 81.3 %all-reduce.12.cloned.1.call-start = ((), (), s32[]{:S(2)}) async-start(), calls=%async_computation.4 | async-start | bytes 131072 | tf_op jit(solution)/shard_map/psum | solution.py:50
  140.3 230.3 %copy-start.1 = (f32[4,32,128]{2,1,0:T(8,128)S(1)}, f32[4,32,128]{2,1,0:T(8,128)}, u32[]{:S(2)}) copy-start(f32[4,32,128]{2,1,0:T(8,128)} %all-reduce.8.cloned.1.call-done) | copy-start | bytes 196612
  143.2 80.2 %all-reduce.14.cloned.1.call-start = ((), (), s32[]{:S(2)}) async-start(), calls=%async_computation.5 | async-start | bytes 131072 | tf_op jit(solution)/shard_map/psum | solution.py:36
  175.0 195.5 %copy-start.2 = (f32[4,32,128]{2,1,0:T(8,128)S(1)}, f32[4,32,128]{2,1,0:T(8,128)}, u32[]{:S(2)}) copy-start(f32[4,32,128]{2,1,0:T(8,128)} %all-reduce.12.cloned.1.call-done) | copy-start | bytes 196612
  191.6 81.3 %all-reduce.16.cloned.1.call-start = ((), (), s32[]{:S(2)}) async-start(), calls=%async_computation.6 | async-start | bytes 131072 | tf_op jit(solution)/shard_map/psum | solution.py:50
  241.0 80.1 %all-reduce.18.cloned.1.call-start = ((), (), s32[]{:S(2)}) async-start(), calls=%async_computation.7 | async-start | bytes 131072 | tf_op jit(solution)/shard_map/psum | solution.py:36
  289.3 81.3 %all-reduce.20.cloned.1.call-start = ((), (), s32[]{:S(2)}) async-start(), calls=%async_computation.8 | async-start | bytes 131072 | tf_op jit(solution)/shard_map/psum | solution.py:50
Sparse Core Ops, SparseCore 0:
  9.6 17.3 reduce-scatter.1
  45.1 32.1 all-reduce.7
  93.8 31.6 all-reduce.9
  143.3 31.6 all-reduce.11
  191.7 31.6 all-reduce.13
  241.1 31.6 all-reduce.15
  289.4 31.6 all-reduce.17
  338.8 31.6 all-reduce.19
where the time goes:
time: 380 us; the launch traced here: 379 us
  waiting for transfers between devices  239 us (63%)
  blocking collectives  97.8 us (26%)
  matrix products  14.9 us (4%)
  between operations  13.6 us (4%)
  other arithmetic  8.02 us (2%)
  local copies, waits for them, and re-layouts  5.16 us (1%)
    psum x4, waiting for transfers between devices, body(): solved_own = lax.psum(partial_solved, 'col')  128 us
    psum x3, waiting for transfers between devices, body(): summed = lax.psum(accumulated[first_row:last_row], 'col')  95.3 us
    all_gather x4, blocking collectives, body(): lax.all_gather(target_rows[:, None], 'row', axis=1, tiled=True)  55.5 us
    all_gather x3, blocking collectives, body(): lax.all_gather(solved_own[:, None], 'row', axis=1, tiled=True)  42.3 us
    reduce_scatter x1, waiting for transfers between devices, body(): lax.psum_scatter(below[0, :, 0], 'layer', scatter_dimension=1, tiled=True)  16.2 us
    dot_general x4, matrix products, body(): jnp.einsum('exnc,xvc->evn', inverted_diagonal[current_supernode], local_t...  11.6 us
  transfers between devices with their start and end apart: 8, of which 8 were waited for; matrix products, arithmetic and copies ran while one was open for 1% of the time, Pallas kernels for 0%

commit v1 on v0

v1 whole, which is shorter than its diff:
```python
import functools

import jax
import jax.numpy as jnp
from jax import lax
from jax.experimental import pallas as pl
from jax.experimental.pallas import tpu as pltpu
from jax.sharding import PartitionSpec as P

F32 = jnp.float32
BF16 = jnp.bfloat16
MESH = pl.DeviceIdType.MESH


def halves(value):
    high = value.astype(BF16)
    return high, (value - high.astype(F32)).astype(BF16)


def stacked(value):
    high, low = halves(value)
    return jnp.concatenate([high.astype(F32), low.astype(F32)], axis=0).astype(BF16)


def dot_nt(left, right):
    return lax.dot_general(
        left, right, (((1,), (1,)), ((), ())), preferred_element_type=F32
    )


def kernel(
    dims,
    right_ref,
    below_ref,
    dinv_ref,
    fac_ref,
    row_ref,
    col_ref,
    out_ref,
    right_v,
    dinv_v,
    fac_v,
    dinv_hi,
    dinv_lo,
    fac_hi,
    fac_lo,
    below_first,
    below_rest,
    part,
    recv_part,
    tb,
    xb,
    recv_t,
    prods,
    *rest,
):
    layers, rows, cols, steps, kr, kc, rhs, blk, nblk = dims
    xs = rest[: steps - 1]
    (
        load_sem,
        y_send,
        y_recv,
        a_send,
        a_recv,
        b_send,
        b_recv,
        o_send,
        o_recv,
    ) = rest[steps - 1 :]
    l = lax.axis_index("layer")
    r = lax.axis_index("row")
    c = lax.axis_index("col")

    def reducers(fn, index=None):
        if kr == cols:
            fn()
        else:
            pl.when((c if index is None else index) < kr)(fn)

    def load_dinv(s):
        return pltpu.make_async_copy(dinv_ref.at[s], dinv_v.at[s], load_sem.at[s])

    load_fac = pltpu.make_async_copy(fac_ref, fac_v, load_sem.at[steps])

    def own_rows(layer):
        return pl.ds(pl.multiple_of(layer * rhs, rhs), rhs)

    def load_right():
        return pltpu.make_async_copy(right_ref.at[:, c], right_v, load_sem.at[steps + 1])

    def load_below(first):
        if first:
            return pltpu.make_async_copy(
                below_ref.at[pl.ds(0, 1), c, own_rows(l)], below_first.at[l], y_recv.at[0, l]
            )
        return pltpu.make_async_copy(
            below_ref.at[pl.ds(1, steps - 1), c, own_rows(l)], below_rest.at[l], y_recv.at[1, l]
        )

    def start_loads():
        load_right().start()
        load_below(True).start()
        load_below(False).start()

    reducers(start_loads)
    load_dinv(0).start()
    load_fac.start()
    for s in range(1, steps):
        load_dinv(s).start()

    barrier = pltpu.get_barrier_semaphore()
    for d in range(1, layers):
        pl.semaphore_signal(
            barrier, inc=1, device_id={"layer": lax.rem(l + d, layers)}, device_id_type=MESH
        )
    for d in range(1, cols):
        pl.semaphore_signal(
            barrier, inc=1, device_id={"col": lax.rem(c + d, cols)}, device_id_type=MESH
        )
    for d in range(1, rows):
        pl.semaphore_signal(
            barrier, inc=1, device_id={"row": lax.rem(r + d, rows), "col": r}, device_id_type=MESH
        )
    for d in range(1, cols):
        pl.semaphore_signal(
            barrier, inc=1, device_id={"row": c, "col": lax.rem(c + d, cols)}, device_id_type=MESH
        )

    @pl.when(c != r)
    def _():
        pl.semaphore_signal(barrier, inc=1, device_id={"col": r}, device_id_type=MESH)
        pl.semaphore_signal(barrier, inc=1, device_id={"row": c}, device_id_type=MESH)

    @pl.when(c != r)
    def _():
        pl.semaphore_wait(barrier, layers - 1 + cols - 1 + cols + rows)

    @pl.when(c == r)
    def _():
        pl.semaphore_wait(barrier, layers - 1 + cols - 1 + (cols - 1) + (rows - 1))

    def y_copy(d, first):
        to = lax.rem(l + d, layers)
        k = 0 if first else 1
        if first:
            src = below_ref.at[pl.ds(0, 1), c, own_rows(to)]
            dst = below_first.at[l]
        else:
            src = below_ref.at[pl.ds(1, steps - 1), c, own_rows(to)]
            dst = below_rest.at[l]
        return pltpu.make_async_remote_copy(
            src_ref=src,
            dst_ref=dst,
            send_sem=y_send.at[k, d],
            recv_sem=y_recv.at[k, l],
            device_id={"layer": to},
            device_id_type=MESH,
        )

    def y_wait(first):
        load_below(first).wait()
        for d in range(1, layers):
            frm = lax.rem(l + d, layers)
            k = 0 if first else 1
            dst = (below_first if first else below_rest).at[frm]
            pltpu.make_async_copy(dst, dst, y_recv.at[k, frm]).wait()

    def start_y():
        for first in (True, False):
            for d in range(1, layers):
                y_copy(d, first).start()

    reducers(start_y)

    def a_copy(ra, d):
        to = lax.rem(c + d, cols)
        return pltpu.make_async_remote_copy(
            src_ref=part.at[ra, lax.rem(to, kr)],
            dst_ref=recv_part.at[ra, c],
            send_sem=a_send.at[ra, d],
            recv_sem=a_recv.at[ra, c],
            device_id={"col": to},
            device_id_type=MESH,
        )

    def a_start(ra):
        for d in range(1, cols):
            reducers(lambda d=d: a_copy(ra, d).start(), lax.rem(c + d, cols))

    def a_sum(ra):
        total = part[ra, lax.rem(c, kr)]
        for d in range(1, cols):
            frm = lax.rem(c + d, cols)
            dst = recv_part.at[ra, frm]
            pltpu.make_async_copy(dst, dst, a_recv.at[ra, frm]).wait()
            total = total + recv_part[ra, frm]
        return total

    def b_buf(rb):
        return recv_t.at[rb // 2] if rb % 2 == 0 else xs[rb // 2]

    def b_copy(rb, d):
        return pltpu.make_async_remote_copy(
            src_ref=(tb if rb % 2 == 0 else xb).at[rb // 2],
            dst_ref=b_buf(rb).at[lax.rem(c, kr)],
            send_sem=b_send.at[rb, d],
            recv_sem=b_recv.at[rb, lax.rem(c, kr)],
            device_id={"row": lax.rem(r + d, rows), "col": r},
            device_id_type=MESH,
        )

    def b_start(rb):
        for d in range(rows - 1, 0, -1):
            b_copy(rb, d).start()

        @pl.when(c != r)
        def _():
            b_copy(rb, 0).start()

        @pl.when(c == r)
        def _():
            pltpu.make_async_copy(
                (tb if rb % 2 == 0 else xb).at[rb // 2],
                b_buf(rb).at[lax.rem(c, kr)],
                b_recv.at[rb, lax.rem(c, kr)],
            ).start()

    def b_wait(rb):
        for i in range(kr):
            dst = b_buf(rb).at[i]
            pltpu.make_async_copy(dst, dst, b_recv.at[rb, i]).wait()

    def o_copy(s, d):
        return pltpu.make_async_remote_copy(
            src_ref=xb.at[s],
            dst_ref=out_ref.at[s * kr + lax.rem(c, kr)],
            send_sem=o_send.at[s, d],
            recv_sem=o_recv.at[s, c],
            device_id={"col": lax.rem(c + d, cols)},
            device_id_type=MESH,
        )

    def o_own(s):
        return pltpu.make_async_copy(
            xb.at[s], out_ref.at[s * kr + lax.rem(c, kr)], o_recv.at[s, c]
        )

    def o_start(s):
        for d in range(1, cols):
            o_copy(s, d).start()
        o_own(s).start()

    def o_wait(s, i):
        dst = out_ref.at[s * kr + lax.rem(i, kr)]
        pltpu.make_async_copy(dst, dst, o_recv.at[s, i]).wait()

    def prepare(s):
        load_dinv(s).wait()
        for i in range(kr):
            for m in range(i + 1):
                high, low = halves(dinv_v[s, i, m])
                dinv_hi[s, i * blk : (i + 1) * blk, m * blk : (m + 1) * blk] = high
                dinv_lo[s, i * blk : (i + 1) * blk, m * blk : (m + 1) * blk] = low

    prepare(0)
    load_fac.wait()
    for n in range(nblk):
        high, low = halves(fac_v[n])
        fac_hi[n] = high
        fac_lo[n] = low
        prods[n] = jnp.zeros((rhs, blk), F32)

    def merged(s):
        value = right_v[s]
        for e in range(layers):
            value = value - (below_first[e, 0] if s == 0 else below_rest[e, s - 1])
        return value

    for s in range(steps):
        def target(s=s):
            if s == 0:
                load_right().wait()
                y_wait(True)
                tb[0] = merged(0)
            else:
                if s == 1:
                    y_wait(False)
                tb[s] = merged(s) - a_sum(2 * s - 1)
            b_start(2 * s)

        reducers(target)
        if s == 0:
            for later in range(1, steps):
                prepare(later)
        b_wait(2 * s)
        pieces = [stacked(recv_t[s, m]) for m in range(kc)]
        for i in range(kr):
            left = jnp.concatenate(pieces[: i + 1], axis=1)
            span = (i + 1) * blk
            rows_of = slice(i * blk, (i + 1) * blk)
            both = dot_nt(left, dinv_hi[s, rows_of, :span]) + dot_nt(
                left, dinv_lo[s, rows_of, :span]
            )
            part[2 * s, i] = both[:rhs] + both[rhs:]
        a_start(2 * s)

        def solved(s=s):
            xb[s] = a_sum(2 * s)
            if s + 1 < steps:
                b_start(2 * s + 1)
            o_start(s)

        reducers(solved)
        if s + 1 == steps:
            break
        b_wait(2 * s + 1)
        sums = [jnp.zeros((rhs, blk), F32) for _ in range(kr)]
        for n in range(nblk):
            place = col_ref[n] // cols - s * kc
            chosen = stacked(xs[s][jnp.clip(place, 0, kc - 1)])
            both = dot_nt(chosen, fac_hi[n]) + dot_nt(chosen, fac_lo[n])
            active = jnp.where((place >= 0) & (place < kc), 1.0, 0.0).astype(F32)
            total = prods[n] + (both[:rhs] + both[rhs:]) * active
            prods[n] = total
            goal = row_ref[n] // rows - (s + 1) * kr
            for i in range(kr):
                sums[i] = sums[i] + total * jnp.where(goal == i, 1.0, 0.0).astype(F32)
        for i in range(kr):
            part[2 * s + 1, i] = sums[i]
        a_start(2 * s + 1)

    for s in range(steps):
        reducers(lambda s=s: o_own(s).wait())
        for d in range(1, cols):
            frm = lax.rem(c + d, cols)
            reducers(lambda s=s, frm=frm: o_wait(s, frm), frm)

    def end_sends():
        for first in (True, False):
            for d in range(1, layers):
                y_copy(d, first).wait_send()
        for rb in range(2 * steps - 1):
            for d in range(1, rows):
                b_copy(rb, d).wait_send()

            @pl.when(c != r)
            def _(rb=rb):
                b_copy(rb, 0).wait_send()

        for s in range(steps):
            for d in range(1, cols):
                o_copy(s, d).wait_send()

    reducers(end_sends)
    for ra in range(2 * steps - 1):
        for d in range(1, cols):
            reducers(lambda ra=ra, d=d: a_copy(ra, d).wait_send(), lax.rem(c + d, cols))


def body(sizes, right_side, below, diag_inverse, factor_blocks, block_row, block_col):
    layers, rows, cols = sizes
    steps, kr, _, kc, _, blk, _ = diag_inverse.shape
    rhs = right_side.shape[2]
    nblk = factor_blocks.shape[2]
    assert rows == cols and kr == kc and kr <= cols
    dims = (layers, rows, cols, steps, kr, kc, rhs, blk, nblk)
    any_space = pl.BlockSpec(memory_space=pl.ANY)
    smem = pl.BlockSpec(memory_space=pltpu.SMEM)
    rounds = 2 * steps - 1
    out = pl.pallas_call(
        functools.partial(kernel, dims),
        out_shape=jax.ShapeDtypeStruct((steps * kr, rhs, blk), F32),
        in_specs=[any_space] * 4 + [smem] * 2,
        out_specs=any_space,
        scratch_shapes=[
            pltpu.VMEM((steps, rhs, blk), F32),
            pltpu.VMEM((steps, kr, kc, blk, blk), F32),
            pltpu.VMEM((nblk, blk, blk), F32),
            pltpu.VMEM((steps, kr * blk, kc * blk), BF16),
            pltpu.VMEM((steps, kr * blk, kc * blk), BF16),
            pltpu.VMEM((nblk, blk, blk), BF16),
            pltpu.VMEM((nblk, blk, blk), BF16),
            pltpu.VMEM((layers, 1, rhs, blk), F32),
            pltpu.VMEM((layers, steps - 1, rhs, blk), F32),
            pltpu.VMEM((rounds, kr, rhs, blk), F32),
            pltpu.VMEM((rounds, cols, rhs, blk), F32),
            pltpu.VMEM((steps, rhs, blk), F32),
            pltpu.VMEM((steps, rhs, blk), F32),
            pltpu.VMEM((steps, kc, rhs, blk), F32),
            pltpu.VMEM((nblk, rhs, blk), F32),
        ]
        + [pltpu.VMEM((kc, rhs, blk), F32) for _ in range(steps - 1)]
        + [
            pltpu.SemaphoreType.DMA((steps + 2,)),
            pltpu.SemaphoreType.DMA((2, layers)),
            pltpu.SemaphoreType.DMA((2, layers)),
            pltpu.SemaphoreType.DMA((rounds, cols)),
            pltpu.SemaphoreType.DMA((rounds, cols)),
            pltpu.SemaphoreType.DMA((rounds, rows)),
            pltpu.SemaphoreType.DMA((rounds, kr)),
            pltpu.SemaphoreType.DMA((steps, cols)),
            pltpu.SemaphoreType.DMA((steps, cols)),
        ],
        compiler_params=pltpu.CompilerParams(collective_id=0, has_side_effects=True),
        name="forward_solve",
    )(
        right_side.reshape(steps, kr, rhs, blk),
        below.reshape(steps, kr, -1, blk),
        diag_inverse.reshape(steps, kr, kc, blk, blk),
        factor_blocks.reshape(nblk, blk, blk),
        block_row.reshape(nblk),
        block_col.reshape(nblk),
    )
    return out.reshape(right_side.shape)


def solution(mesh):
    sizes = tuple(mesh.shape[name] for name in ("layer", "row", "col"))
    return jax.shard_map(
        functools.partial(body, sizes),
        mesh=mesh,
        in_specs=(
            P(None, "row", "layer", None),
            P("layer", None, "row", None, None),
            P(None, None, "row", None, "col", None, None),
            P("row", "col", None, None, None),
            P("row", "col", None),
            P("row", "col", None),
        ),
        out_specs=P(None, "row", "layer", None),
        check_vma=False,
    )
```

time: 380 us -> 61.1 us (0.16)
  waiting for transfers between devices: 239 us -> 0 us
  blocking collectives: 97.8 us -> 0 us
  Pallas kernels: 0 us -> 59.2 us
  matrix products: 14.9 us -> 0 us
  between operations: 13.6 us -> 0.01 us
  other arithmetic: 8.02 us -> 0 us
    psum x7 -> x0, waiting for transfers between devices: 223 us -> none  [the longest x4 128 us: body(): solved_own = lax.psum(partial_solved, 'col')]
    all_gather x7 -> x0, blocking collectives: 97.8 us -> none  [the longest x4 55.5 us: body(): lax.all_gather(target_rows[:, None], 'row', axis=1, tiled=True)]
    pallas_call x0 -> x1, Pallas kernels: none -> 59.2 us  [body(): pl.pallas_call(functools.partial(kernel, dims), out_shape=jax.ShapeDtypeS...]
    reduce_scatter x1 -> x0, waiting for transfers between devices: 16.2 us -> none  [body(): lax.psum_scatter(below[0, :, 0], 'layer', scatter_dimension=1, tiled=True)]
    dot_general x10 -> x0, matrix products: 14.9 us -> none  [the longest x4 11.6 us: body(): jnp.einsum('exnc,xvc->evn', inverted_diagonal[current_supernode], local_t...]
  transfers between devices with their start and end apart: 8 -> 0, of which waited for: 8 -> 0; matrix products, arithmetic and copies ran while one was open for 1% -> 0% of each run, Pallas kernels for 0% -> 0%
where the time goes in v1:
time: 61.1 us; the launch traced here: 60.9 us
  Pallas kernels  59.2 us (97%)
  local copies, waits for them, and re-layouts  1.67 us (3%)
    pallas_call x1, Pallas kernels, body(): pl.pallas_call(functools.partial(kernel, dims), out_shape=jax.ShapeDtypeS...  59.2 us
    unnamed x1, local copies, waits for them, and re-layouts  1.67 us

profile of v1, /device:TPU:0, one launch (start us, length us, event | category | flops | bytes accessed | tf_op | source)
XLA Modules:
  0.0 60.9 jit_solution(17928523112544729189)
XLA Ops:
  0.0 59.2 %forward_solve.1 = f32[16,32,128]{2,1,0:T(8,128)} custom-call(f32[4,4,32,128]{3,2,1,0:T(8,128)} %bitcast.12, f32[4,4,64,128]{3,2,1,0:T(8,128)} %bitcast.11, f32[4,4,4,128,128]{4,3,2,1,0:T(8,128)} %bitcast.9, f32[4,128,128]{2,1,0:T(8,128)} %bitcast.13, s32[4]{0:T(128)} %bitcast.14, s32[4]{0:T(128)} %bitcast.15), custom_call_target="tpu_custom_call" | custom-call | tf_op jit(solution)/shard_map/forward_solve/pallas_call | solution.py:370
  59.2 1.7 %copy.9 = f32[16,1,32,128]{3,2,1,0:T(8,128)} copy(f32[16,1,32,128]{3,2,1,0:T(8,128)} %bitcast.10) | data formatting | bytes 524288

commit v2 on v1

--- a/solution.py
+++ b/solution.py
@@ -22,9 +22,9 @@
     return jnp.concatenate([high.astype(F32), low.astype(F32)], axis=0).astype(BF16)
 
 
-def dot_nt(left, right):
+def dot_nn(left, right):
     return lax.dot_general(
-        left, right, (((1,), (1,)), ((), ())), preferred_element_type=F32
+        left, right, (((1,), (0,)), ((), ())), preferred_element_type=F32
     )
 
 
@@ -49,9 +49,11 @@
     part,
     recv_part,
     tb,
-    xb,
     recv_t,
     prods,
+    terms,
+    psum,
+    oterms,
     *rest,
 ):
     layers, rows, cols, steps, kr, kc, rhs, blk, nblk = dims
@@ -64,6 +66,8 @@
         a_recv,
         b_send,
         b_recv,
+        d_send,
+        d_recv,
         o_send,
         o_recv,
     ) = rest[steps - 1 :]
@@ -172,100 +176,127 @@
 
     reducers(start_y)
 
-    def a_copy(ra, d):
-        to = lax.rem(c + d, cols)
+    half = lax.rem(c, 2)
+    hk = kr // 2
+
+    def p_copy(ra):
         return pltpu.make_async_remote_copy(
-            src_ref=part.at[ra, lax.rem(to, kr)],
-            dst_ref=recv_part.at[ra, c],
-            send_sem=a_send.at[ra, d],
-            recv_sem=a_recv.at[ra, c],
-            device_id={"col": to},
+            src_ref=part.at[ra, pl.ds((1 - half) * hk, hk)],
+            dst_ref=recv_part.at[ra],
+            send_sem=a_send.at[ra],
+            recv_sem=a_recv.at[ra],
+            device_id={"col": c + 1 - 2 * half},
             device_id_type=MESH,
         )
 
-    def a_start(ra):
-        for d in range(1, cols):
-            reducers(lambda d=d: a_copy(ra, d).start(), lax.rem(c + d, cols))
-
-    def a_sum(ra):
-        total = part[ra, lax.rem(c, kr)]
-        for d in range(1, cols):
-            frm = lax.rem(c + d, cols)
-            dst = recv_part.at[ra, frm]
-            pltpu.make_async_copy(dst, dst, a_recv.at[ra, frm]).wait()
-            total = total + recv_part[ra, frm]
-        return total
-
-    def b_buf(rb):
-        return recv_t.at[rb // 2] if rb % 2 == 0 else xs[rb // 2]
-
-    def b_copy(rb, d):
+    def p_sum(ra):
+        p_copy(ra).start()
+        pltpu.make_async_copy(recv_part.at[ra], recv_part.at[ra], a_recv.at[ra]).wait()
+        psum[ra] = part[ra, pl.ds(half * hk, hk)] + recv_part[ra]
+
+    def over_pairs(ref, index):
+        blocks = []
+        for i in range(kr):
+            h, j = i // hk, i % hk
+            total = ref[index, h, j]
+            for e in range(2, cols, 2):
+                total = total + ref[index, e + h, j]
+            blocks.append(total)
+        return blocks
+
+    def b_copy(d):
         return pltpu.make_async_remote_copy(
-            src_ref=(tb if rb % 2 == 0 else xb).at[rb // 2],
-            dst_ref=b_buf(rb).at[lax.rem(c, kr)],
-            send_sem=b_send.at[rb, d],
-            recv_sem=b_recv.at[rb, lax.rem(c, kr)],
+            src_ref=tb,
+            dst_ref=recv_t.at[lax.rem(c, kr)],
+            send_sem=b_send.at[d],
+            recv_sem=b_recv.at[lax.rem(c, kr)],
             device_id={"row": lax.rem(r + d, rows), "col": r},
             device_id_type=MESH,
         )
 
-    def b_start(rb):
+    def b_start():
         for d in range(rows - 1, 0, -1):
-            b_copy(rb, d).start()
+            b_copy(d).start()
 
         @pl.when(c != r)
         def _():
-            b_copy(rb, 0).start()
+            b_copy(0).start()
 
         @pl.when(c == r)
         def _():
             pltpu.make_async_copy(
-                (tb if rb % 2 == 0 else xb).at[rb // 2],
-                b_buf(rb).at[lax.rem(c, kr)],
-                b_recv.at[rb, lax.rem(c, kr)],
+                tb, recv_t.at[lax.rem(c, kr)], b_recv.at[lax.rem(c, kr)]
             ).start()
 
-    def b_wait(rb):
-        for i in range(kr):
-            dst = b_buf(rb).at[i]
-            pltpu.make_async_copy(dst, dst, b_recv.at[rb, i]).wait()
+    def b_wait():
+        for i in range(kr):
+            dst = recv_t.at[i]
+            pltpu.make_async_copy(dst, dst, b_recv.at[i]).wait()
+
+    def d_copy(ra, d):
+        return pltpu.make_async_remote_copy(
+            src_ref=psum.at[ra],
+            dst_ref=terms.at[ra, c],
+            send_sem=d_send.at[ra, d],
+            recv_sem=d_recv.at[ra, c],
+            device_id={"row": lax.rem(r + d, rows), "col": r},
+            device_id_type=MESH,
+        )
+
+    def d_start(ra):
+        for d in range(rows - 1, 0, -1):
+            d_copy(ra, d).start()
+
+        @pl.when(c != r)
+        def _():
+            d_copy(ra, 0).start()
+
+        @pl.when(c == r)
+        def _():
+            pltpu.make_async_copy(psum.at[ra], terms.at[ra, c], d_recv.at[ra, c]).start()
+
+    def d_sum(ra):
+        for e in range(cols):
+            dst = terms.at[ra, e]
+            pltpu.make_async_copy(dst, dst, d_recv.at[ra, e]).wait()
+        return over_pairs(terms, ra)
 
     def o_copy(s, d):
         return pltpu.make_async_remote_copy(
-            src_ref=xb.at[s],
-            dst_ref=out_ref.at[s * kr + lax.rem(c, kr)],
+            src_ref=psum.at[2 * s],
+            dst_ref=oterms.at[s, c],
             send_sem=o_send.at[s, d],
             recv_sem=o_recv.at[s, c],
             device_id={"col": lax.rem(c + d, cols)},
             device_id_type=MESH,
         )
 
-    def o_own(s):
-        return pltpu.make_async_copy(
-            xb.at[s], out_ref.at[s * kr + lax.rem(c, kr)], o_recv.at[s, c]
-        )
-
     def o_start(s):
         for d in range(1, cols):
             o_copy(s, d).start()
-        o_own(s).start()
-
-    def o_wait(s, i):
-        dst = out_ref.at[s * kr + lax.rem(i, kr)]
-        pltpu.make_async_copy(dst, dst, o_recv.at[s, i]).wait()
+        oterms[s, c] = psum[2 * s]
+
+    def o_finish(s):
+        for d in range(1, cols):
+            frm = lax.rem(c + d, cols)
+            dst = oterms.at[s, frm]
+            pltpu.make_async_copy(dst, dst, o_recv.at[s, frm]).wait()
+        blocks = over_pairs(oterms, s)
+        for i in range(kr):
+            out_ref[s * kr + i] = blocks[i]
 
     def prepare(s):
         load_dinv(s).wait()
         for i in range(kr):
             for m in range(i + 1):
-                high, low = halves(dinv_v[s, i, m])
-                dinv_hi[s, i * blk : (i + 1) * blk, m * blk : (m + 1) * blk] = high
-                dinv_lo[s, i * blk : (i + 1) * blk, m * blk : (m + 1) * blk] = low
+                high, low = halves(dinv_v[s, i, m].T)
+                dinv_hi[s, m * blk : (m + 1) * blk, i * blk : (i + 1) * blk] = high
+                dinv_lo[s, m * blk : (m + 1) * blk, i * blk : (i + 1) * blk] = low
 
     prepare(0)
     load_fac.wait()
     for n in range(nblk):
-        high, low = halves(fac_v[n])
+        high, low = halves(fac_v[n].T)
         fac_hi[n] = high
         fac_lo[n] = low
         prods[n] = jnp.zeros((rhs, blk), F32)
@@ -276,85 +307,89 @@
             value = value - (below_first[e, 0] if s == 0 else below_rest[e, s - 1])
         return value
 
+    def first_target():
+        load_right().wait()
+        y_wait(True)
+        tb[...] = merged(0)
+        b_start()
+
+    reducers(first_target)
+    b_wait()
+    goals = [recv_t[m] for m in range(kc)]
     for s in range(steps):
-        def target(s=s):
-            if s == 0:
-                load_right().wait()
-                y_wait(True)
-                tb[0] = merged(0)
-            else:
-                if s == 1:
-                    y_wait(False)
-                tb[s] = merged(s) - a_sum(2 * s - 1)
-            b_start(2 * s)
-
-        reducers(target)
-        if s == 0:
-            for later in range(1, steps):
-                prepare(later)
-        b_wait(2 * s)
-        pieces = [stacked(recv_t[s, m]) for m in range(kc)]
+        pieces = [stacked(value) for value in goals]
         for i in range(kr):
             left = jnp.concatenate(pieces[: i + 1], axis=1)
             span = (i + 1) * blk
             rows_of = slice(i * blk, (i + 1) * blk)
-            both = dot_nt(left, dinv_hi[s, rows_of, :span]) + dot_nt(
-                left, dinv_lo[s, rows_of, :span]
+            both = dot_nn(left, dinv_hi[s, :span, rows_of]) + dot_nn(
+                left, dinv_lo[s, :span, rows_of]
             )
             part[2 * s, i] = both[:rhs] + both[rhs:]
-        a_start(2 * s)
-
-        def solved(s=s):
-            xb[s] = a_sum(2 * s)
-            if s + 1 < steps:
-                b_start(2 * s + 1)
-            o_start(s)
-
-        reducers(solved)
+        p_sum(2 * s)
+        if s + 1 < steps:
+            d_start(2 * s)
+        o_start(s)
+        if s + 1 < steps:
+            prepare(s + 1)
         if s + 1 == steps:
             break
-        b_wait(2 * s + 1)
+        found = d_sum(2 * s)
+        for m in range(kc):
+            xs[s][m] = found[m]
         sums = [jnp.zeros((rhs, blk), F32) for _ in range(kr)]
         for n in range(nblk):
             place = col_ref[n] // cols - s * kc
             chosen = stacked(xs[s][jnp.clip(place, 0, kc - 1)])
-            both = dot_nt(chosen, fac_hi[n]) + dot_nt(chosen, fac_lo[n])
+            both = dot_nn(chosen, fac_hi[n]) + dot_nn(chosen, fac_lo[n])
             active = jnp.where((place >= 0) & (place < kc), 1.0, 0.0).astype(F32)
             total = prods[n] + (both[:rhs] + both[rhs:]) * active
             prods[n] = total
             goal = row_ref[n] // rows - (s + 1) * kr
             for i in range(kr):
-                sums[i] = sums[i] + total * jnp.where(goal == i, 1.0, 0.0).astype(F32)
+                sums[i] = sums[i] - total * jnp.where(goal == i, 1.0, 0.0).astype(F32)
         for i in range(kr):
             part[2 * s + 1, i] = sums[i]
-        a_start(2 * s + 1)
-
-    for s in range(steps):
-        reducers(lambda s=s: o_own(s).wait())
-        for d in range(1, cols):
-            frm = lax.rem(c + d, cols)
-            reducers(lambda s=s, frm=frm: o_wait(s, frm), frm)
+
+        def add_merged(s=s):
+            if s == 0:
+                y_wait(False)
+            mine = lax.rem(c, kr)
+            part[2 * s + 1, mine] = part[2 * s + 1, mine] + merged(s + 1)
+
+        reducers(add_merged)
+        p_sum(2 * s + 1)
+        d_start(2 * s + 1)
+        o_finish(s)
+        found = d_sum(2 * s + 1)
+        goals = [found[m] for m in range(kc)]
+
+    o_finish(steps - 1)
 
     def end_sends():
         for first in (True, False):
             for d in range(1, layers):
                 y_copy(d, first).wait_send()
-        for rb in range(2 * steps - 1):
-            for d in range(1, rows):
-                b_copy(rb, d).wait_send()
-
-            @pl.when(c != r)
-            def _(rb=rb):
-                b_copy(rb, 0).wait_send()
-
-        for s in range(steps):
-            for d in range(1, cols):
-                o_copy(s, d).wait_send()
+        for d in range(1, rows):
+            b_copy(d).wait_send()
+
+        @pl.when(c != r)
+        def _():
+            b_copy(0).wait_send()
 
     reducers(end_sends)
     for ra in range(2 * steps - 1):
+        p_copy(ra).wait_send()
+    for s in range(steps):
         for d in range(1, cols):
-            reducers(lambda ra=ra, d=d: a_copy(ra, d).wait_send(), lax.rem(c + d, cols))
+            o_copy(s, d).wait_send()
+    for ra in range(2 * steps - 2):
+        for d in range(1, rows):
+            d_copy(ra, d).wait_send()
+
+        @pl.when(c != r)
+        def _(ra=ra):
+            d_copy(ra, 0).wait_send()
 
 
 def body(sizes, right_side, below, diag_inverse, factor_blocks, block_row, block_col):
@@ -362,42 +397,46 @@
     steps, kr, _, kc, _, blk, _ = diag_inverse.shape
     rhs = right_side.shape[2]
     nblk = factor_blocks.shape[2]
-    assert rows == cols and kr == kc and kr <= cols
+    assert rows == cols and kr == kc and kr <= cols and kr % 2 == 0 and cols % 2 == 0
     dims = (layers, rows, cols, steps, kr, kc, rhs, blk, nblk)
     any_space = pl.BlockSpec(memory_space=pl.ANY)
     smem = pl.BlockSpec(memory_space=pltpu.SMEM)
     rounds = 2 * steps - 1
     out = pl.pallas_call(
         functools.partial(kernel, dims),
-        out_shape=jax.ShapeDtypeStruct((steps * kr, rhs, blk), F32),
+        out_shape=pltpu.VMEM((steps * kr, rhs, blk), F32),
         in_specs=[any_space] * 4 + [smem] * 2,
-        out_specs=any_space,
+        out_specs=pl.BlockSpec(memory_space=pltpu.VMEM),
         scratch_shapes=[
             pltpu.VMEM((steps, rhs, blk), F32),
             pltpu.VMEM((steps, kr, kc, blk, blk), F32),
             pltpu.VMEM((nblk, blk, blk), F32),
-            pltpu.VMEM((steps, kr * blk, kc * blk), BF16),
-            pltpu.VMEM((steps, kr * blk, kc * blk), BF16),
+            pltpu.VMEM((steps, kc * blk, kr * blk), BF16),
+            pltpu.VMEM((steps, kc * blk, kr * blk), BF16),
             pltpu.VMEM((nblk, blk, blk), BF16),
             pltpu.VMEM((nblk, blk, blk), BF16),
             pltpu.VMEM((layers, 1, rhs, blk), F32),
             pltpu.VMEM((layers, steps - 1, rhs, blk), F32),
             pltpu.VMEM((rounds, kr, rhs, blk), F32),
-            pltpu.VMEM((rounds, cols, rhs, blk), F32),
-            pltpu.VMEM((steps, rhs, blk), F32),
-            pltpu.VMEM((steps, rhs, blk), F32),
-            pltpu.VMEM((steps, kc, rhs, blk), F32),
+            pltpu.VMEM((rounds, kr // 2, rhs, blk), F32),
+            pltpu.VMEM((rhs, blk), F32),
+            pltpu.VMEM((kc, rhs, blk), F32),
             pltpu.VMEM((nblk, rhs, blk), F32),
+            pltpu.VMEM((rounds - 1, cols, kr // 2, rhs, blk), F32),
+            pltpu.VMEM((rounds, kr // 2, rhs, blk), F32),
+            pltpu.VMEM((steps, cols, kr // 2, rhs, blk), F32),
         ]
         + [pltpu.VMEM((kc, rhs, blk), F32) for _ in range(steps - 1)]
         + [
             pltpu.SemaphoreType.DMA((steps + 2,)),
             pltpu.SemaphoreType.DMA((2, layers)),
             pltpu.SemaphoreType.DMA((2, layers)),
-            pltpu.SemaphoreType.DMA((rounds, cols)),
-            pltpu.SemaphoreType.DMA((rounds, cols)),
-            pltpu.SemaphoreType.DMA((rounds, rows)),
-            pltpu.SemaphoreType.DMA((rounds, kr)),
+            pltpu.SemaphoreType.DMA((rounds,)),
+            pltpu.SemaphoreType.DMA((rounds,)),
+            pltpu.SemaphoreType.DMA((rows,)),
+            pltpu.SemaphoreType.DMA((kr,)),
+            pltpu.SemaphoreType.DMA((rounds - 1, rows)),
+            pltpu.SemaphoreType.DMA((rounds - 1, cols)),
             pltpu.SemaphoreType.DMA((steps, cols)),
             pltpu.SemaphoreType.DMA((steps, cols)),
         ],

time: 61.1 us -> 56.2 us (0.920)
  Pallas kernels: 59.2 us -> 55.3 us
  local copies, waits for them, and re-layouts: 1.67 us -> 0.71 us
    pallas_call x1, Pallas kernels: 59.2 us -> 55.3 us  [body(): pl.pallas_call(functools.partial(kernel, dims), out_shape=pltpu.VMEM((ste...]
    unnamed x1, local copies, waits for them, and re-layouts: 1.67 us -> 0.71 us
where the time goes in v2:
time: 56.2 us; the launch traced here: 56 us
  Pallas kernels  55.3 us (98%)
  local copies, waits for them, and re-layouts  0.71 us (1%)
    pallas_call x1, Pallas kernels, body(): pl.pallas_call(functools.partial(kernel, dims), out_shape=pltpu.VMEM((ste...  55.3 us

profile of v2, /device:TPU:0, one launch (start us, length us, event | category | flops | bytes accessed | tf_op | source)
XLA Modules:
  0.0 56.0 jit_solution(7610215417396475934)
XLA Ops:
  0.0 55.3 %forward_solve.1 = f32[16,32,128]{2,1,0:T(8,128)S(1)} custom-call(f32[4,4,32,128]{3,2,1,0:T(8,128)} %bitcast.12, f32[4,4,64,128]{3,2,1,0:T(8,128)} %bitcast.11, f32[4,4,4,128,128]{4,3,2,1,0:T(8,128)} %bitcast.10, f32[4,128,128]{2,1,0:T(8,128)} %bitcast.13, s32[4]{0:T(128)} %bitcast.14, s32[4]{0:T(128)} %bitcast.15), custom_call_target="tpu_custom_call" | custom-call | tf_op jit(solution)/shard_map/forward_solve/pallas_call | solution.py:405
  55.3 0.7 %copy.9 = f32[16,1,32,128]{3,2,1,0:T(8,128)} copy(f32[16,1,32,128]{3,2,1,0:T(8,128)S(1)} %bitcast.9) | data formatting | bytes 524288
